TPU v7x, 32 devices: a whole 2x2x4 slice. The times are simulated.
32 devices in a mesh: dp: 8 (over z, y), tensor: 4 (over x, core).
Axes of the slice: x: 2, y: 2, z: 4, core: 2. Of those that a mesh axis runs over, the one named last changes fastest.
Arguments:
- layer_input: bfloat16 [196, 64, 768], P('tensor', 'dp'), may hold values from -6 to 6
- image_counts: int32 [8], P('dp'), may hold values from 4 to 8
- expand: bfloat16 [196, 384], P(None, 'tensor'), may hold values from -0.4375 to 0.4375
- uplift: bfloat16 [384], P('tensor'), may hold values from -3 to 3
- contract: bfloat16 [384, 196], P('tensor'), may hold values from -0.3125 to 0.3125
- offset: bfloat16 [196], P('tensor'), may hold values from -3 to 3
- scaling: bfloat16 [768], replicated, may hold values from 0.099609375 to 1.8984375
- centering: bfloat16 [768], replicated, may hold values from -3 to 3
- rescaling: bfloat16 [768], replicated, may hold values from 0.099609375 to 1.8984375
- recentering: bfloat16 [768], replicated, may hold values from -3 to 3
- broaden: bfloat16 [768, 3072], replicated, may hold values from -0.21875 to 0.21875
- raising: bfloat16 [3072], replicated, may hold values from -3 to 3
- narrow: bfloat16 [3072, 768], replicated, may hold values from -0.109375 to 0.109375
- lowering: bfloat16 [768], replicated, may hold values from -3 to 3
- cotangent: bfloat16 [196, 64, 768], P('tensor', 'dp'), may hold values from -6 to 6
Outputs:
- layer_output: bfloat16 [196, 64, 768], P('tensor', 'dp')
- input_grad: bfloat16 [196, 64, 768], P('tensor', 'dp')
- expand_grad: float32 [196, 384], P(None, 'tensor')
- uplift_grad: float32 [384], P('tensor')
- contract_grad: float32 [384, 196], P('tensor')
- offset_grad: float32 [196], P('tensor')
- scaling_grad: float32 [768], replicated
- centering_grad: float32 [768], replicated
- rescaling_grad: float32 [768], replicated
- recentering_grad: float32 [768], replicated
- broaden_grad: float32 [768, 3072], P(None, ('dp', 'tensor'))
- raising_grad: float32 [3072], P(('dp', 'tensor'))
- narrow_grad: float32 [3072, 768], P(('dp', 'tensor'))
- lowering_grad: float32 [768], replicated
Inputs may be any that keep to these rules, and one draw needn't show every extreme that they name: `image_counts`: slots of a dp index at or above its count hold padding images.
All inputs are finite; a program needn't handle non-finite values.
Results may differ from a plain program's by a relative error of at most 0.007.
Values may be sent and summed in bfloat16 or wider, within the bound.
A program may use at most 128 MiB of HBM per device.

v0:
```python
import jax
import jax.numpy as jnp
from jax import lax
from jax.sharding import PartitionSpec as P


def layer_norm(values, scale_vec, shift_vec):
    centre = values - jnp.mean(values, axis=-1, keepdims=True)
    spread = jnp.mean(centre * centre, axis=-1, keepdims=True)
    return centre * lax.rsqrt(spread + 1e-06) * scale_vec + shift_vec


def local(
    layer_input,
    image_counts,
    expand,
    uplift,
    contract,
    offset,
    scaling,
    centering,
    rescaling,
    recentering,
    broaden,
    raising,
    narrow,
    lowering,
    cotangent,
):
    part_rows, images, model_width = layer_input.shape
    columns = images * model_width
    image_mask = (jnp.arange(images, dtype=jnp.int32) < image_counts[0]).astype(jnp.float32)
    row_mask = jnp.tile(image_mask, part_rows)[:, None]
    input_float = layer_input.astype(jnp.float32)
    normed_first, first_back = jax.vjp(
        layer_norm, input_float, scaling.astype(jnp.float32), centering.astype(jnp.float32)
    )
    normed_local = normed_first.astype(jnp.bfloat16).reshape(part_rows, columns)
    normed_all = lax.all_gather(normed_local, "tensor", axis=0, tiled=True)
    token_pre = (
        jnp.einsum("sj,sn->jn", expand, normed_all, preferred_element_type=jnp.float32)
        + uplift.astype(jnp.float32)[:, None]
    )
    token_act, gelu_token = jax.vjp(jax.nn.gelu, token_pre)
    token_low = token_act.astype(jnp.bfloat16)
    weight_block = contract
    token_out = lax.psum_scatter(
        jnp.einsum("js,jn->sn", weight_block, token_low, preferred_element_type=jnp.float32),
        "tensor",
        scatter_dimension=0,
        tiled=True,
    )
    token_out = token_out + offset.astype(jnp.float32)[:, None]
    mixed_rows = input_float.reshape(part_rows * images, model_width) + token_out.reshape(
        part_rows * images, model_width
    )
    normed_second, second_back = jax.vjp(
        layer_norm, mixed_rows, rescaling.astype(jnp.float32), recentering.astype(jnp.float32)
    )
    normed_low = normed_second.astype(jnp.bfloat16)
    channel_pre = jnp.dot(normed_low, broaden, preferred_element_type=jnp.float32) + raising.astype(
        jnp.float32
    )
    channel_act, gelu_channel = jax.vjp(jax.nn.gelu, channel_pre)
    channel_low = channel_act.astype(jnp.bfloat16)
    channel_out = jnp.dot(
        channel_low, narrow, preferred_element_type=jnp.float32
    ) + lowering.astype(jnp.float32)
    layer_output = (
        ((mixed_rows + channel_out) * row_mask)
        .astype(jnp.bfloat16)
        .reshape(part_rows, images, model_width)
    )
    out_grad = cotangent.astype(jnp.float32).reshape(part_rows * images, model_width) * row_mask
    out_low = out_grad.astype(jnp.bfloat16)
    narrow_grad = jnp.einsum("rk,rd->kd", channel_low, out_low, preferred_element_type=jnp.float32)
    lowering_grad = jnp.sum(out_low.astype(jnp.float32), axis=0)
    act_grad = jnp.einsum("rd,kd->rk", out_low, narrow, preferred_element_type=jnp.float32)
    (pre_grad,) = gelu_channel(act_grad)
    pre_low = pre_grad.astype(jnp.bfloat16)
    broaden_grad = jnp.einsum("rd,rk->dk", normed_low, pre_low, preferred_element_type=jnp.float32)
    raising_grad = jnp.sum(pre_low.astype(jnp.float32), axis=0)
    normed_grad = jnp.einsum("rk,dk->rd", pre_low, broaden, preferred_element_type=jnp.float32)
    rows_grad, rescaling_grad, recentering_grad = second_back(normed_grad)
    mixed_grad = out_grad + rows_grad
    mixed_low = mixed_grad.astype(jnp.bfloat16).reshape(part_rows, columns)
    offset_grad = jnp.sum(mixed_low.astype(jnp.float32), axis=1)
    mixed_all = lax.all_gather(mixed_low, "tensor", axis=0, tiled=True)
    act_token_grad = jnp.einsum(
        "js,sn->jn", contract, mixed_all, preferred_element_type=jnp.float32
    )
    (token_grad,) = gelu_token(act_token_grad)
    token_grad_low = token_grad.astype(jnp.bfloat16)
    expand_grad = jnp.einsum(
        "sn,jn->sj", normed_all, token_grad_low, preferred_element_type=jnp.float32
    )
    contract_grad = jnp.einsum(
        "jn,sn->js", token_low, mixed_all, preferred_element_type=jnp.float32
    )
    uplift_grad = jnp.sum(token_grad_low.astype(jnp.float32), axis=1)
    weight_block = expand
    normed_back = lax.psum_scatter(
        jnp.einsum("sj,jn->sn", weight_block, token_grad_low, preferred_element_type=jnp.float32),
        "tensor",
        scatter_dimension=0,
        tiled=True,
    )
    input_back, scaling_grad, centering_grad = first_back(
        normed_back.reshape(part_rows, images, model_width)
    )
    input_grad = (mixed_grad.reshape(part_rows, images, model_width) + input_back).astype(
        jnp.bfloat16
    )
    expand_grad, uplift_grad, contract_grad, offset_grad = lax.psum(
        (expand_grad, uplift_grad, contract_grad, offset_grad), "dp"
    )
    lowering_grad, scaling_grad, centering_grad, rescaling_grad, recentering_grad = lax.psum(
        (lowering_grad, scaling_grad, centering_grad, rescaling_grad, recentering_grad),
        ("dp", "tensor"),
    )
    broaden_grad, narrow_grad, raising_grad = (
        lax.psum_scatter(broaden_grad, ("dp", "tensor"), scatter_dimension=1, tiled=True),
        lax.psum_scatter(narrow_grad, ("dp", "tensor"), scatter_dimension=0, tiled=True),
        lax.psum_scatter(raising_grad, ("dp", "tensor"), scatter_dimension=0, tiled=True),
    )
    return (
        layer_output,
        input_grad,
        expand_grad,
        uplift_grad,
        contract_grad,
        offset_grad,
        scaling_grad,
        centering_grad,
        rescaling_grad,
        recentering_grad,
        broaden_grad,
        raising_grad,
        narrow_grad,
        lowering_grad,
    )


def solution(mesh):
    in_specs = (
        P("tensor", "dp", None),
        P("dp"),
        P(None, "tensor"),
        P("tensor"),
        P("tensor", None),
        P("tensor"),
        P(),
        P(),
        P(),
        P(),
        P(),
        P(),
        P(),
        P(),
        P("tensor", "dp", None),
    )
    out_specs = (
        P("tensor", "dp", None),
        P("tensor", "dp", None),
        P(None, "tensor"),
        P("tensor"),
        P("tensor", None),
        P("tensor"),
        P(),
        P(),
        P(),
        P(),
        P(None, ("dp", "tensor")),
        P(("dp", "tensor")),
        P(("dp", "tensor"), None),
        P(),
    )
    return jax.shard_map(local, mesh=mesh, in_specs=in_specs, out_specs=out_specs, check_vma=False)
```

profile of v0, /device:TPU:0, one launch (start us, length us, event | category | flops | bytes accessed | tf_op | source)
XLA Modules:
  0.0 556.1 jit_solution(4556848983229731333)
XLA Ops:
  13.9 29.1 %all-gather.5.cloned.1.call-done = bf16[4,49,6144]{2,1,0:T(8,128)(2,1)} async-done(((bf16[1,49,6144]{2,1,0:T(8,128)(2,1)}), bf16[4,49,6144]{2,1,0:T(8,128)(2,1)}) %all-gather.5.cloned.1.call-update) | async-done | bytes 2408464 | tf_op jit(solution)/shard_map/all_gather | solution.py:39
  42.9 2.5 reshape.166
  47.4 3.1 convolution_bitcast_fusion.1
  50.6 51.8 %fusion = f32[56,6144]{1,0:T(8,128)} fusion(f32[196,6144]{1,0:T(8,128)} %convolution_bitcast_fusion.1), kind=kCustom, calls=%all-reduce-scatter | all-reduce-scatter fusion | flops 1376257 | bytes 6193664
  107.7 8.4 %concatenate = f32[77,6144]{1,0:T(8,128)} concatenate(f32[21,6144]{1,0:T(8,128)} %collective-permute-done, f32[56,6144]{1,0:T(8,128)} %fusion), dimensions={0} | concatenate | bytes 3784704
  116.1 2.7 dynamic-slice_add_fusion
  118.8 2.6 reshape.158
  126.4 4.5 fusion.52
  131.0 5.4 convert_reduce_fusion
  136.5 2.4 multiply_reduce_fusion
  144.2 34.2 %all-gather.7.cloned.1.call-done = bf16[4,49,6144]{2,1,0:T(8,128)(2,1)} async-done(((bf16[1,49,6144]{2,1,0:T(8,128)(2,1)}), bf16[4,49,6144]{2,1,0:T(8,128)(2,1)}) %all-gather.7.cloned.1.call-update) | async-done | bytes 2408464 | tf_op jit(solution)/shard_map/all_gather | solution.py:88
  178.4 4.0 reshape.168
  182.4 4.3 fusion.48
  191.6 9.4 %fusion.41 = f32[3072,768]{1,0:T(8,128)} fusion(bf16[49,8,768]{2,1,0:T(8,128)(2,1)} %param.29, f32[392]{0:T(512)S(1)} %mul.240, f32[392,3072]{1,0:T(8,128)} %copy-done.25, f32[3072]{0:T(1024)S(1)} %convert_element_type.94), kind=kOutput, calls=%fused_computation.69 | convolution fusion | flops 1862633472 | bytes 14870048 | tf_op jit(solution)/shard_map/rk,rd->kd/dot_general | solution.py:76
  202.1 8.0 %fusion.54 = f32[768,3072]{0,1:T(8,128)} fusion(bf16[392,768]{1,0:T(8,128)(2,1)S(1)} %copy-done.15, bf16[392,3072]{1,0:T(8,128)(2,1)} %copy-done.24), kind=kOutput, calls=%fused_computation.87 | convolution fusion | flops 1849688064 | bytes 12447744 | tf_op jit(solution)/shard_map/rd,rk->dk/dot_general | solution.py:81
  211.3 3.1 convolution_bitcast_fusion
  214.4 51.0 %fusion.1 = f32[56,6144]{1,0:T(8,128)S(1)} fusion(f32[196,6144]{1,0:T(8,128)} %convolution_bitcast_fusion), kind=kCustom, calls=%all-reduce-scatter.1 | all-reduce-scatter fusion | flops 1376257 | bytes 6193664
  266.3 2.4 collective-permute-start.1
  268.6 7.7 %fusion.26 = bf16[49,8,768]{2,1,0:T(8,128)(2,1)} fusion(bf16[3072,768]{1,0:T(8,128)(2,1)} %param.27, f32[392]{0:T(512)S(1)} %mul.240, f32[768]{0:T(1024)S(1)} %convert_element_type.96, f32[392,768]{1,0:T(8,128)S(1)} %copy-done.6, bf16[49,8,768]{2,1,0:T(8,128)(2,1)S(1)} %copy-done.2, f32[392,3072]{1,0:T(8,128)} %copy-done.25, f32[3072]{0:T(1024)S(1)} %convert_element_type.94), kind=kOutput, calls=%fused_computation.46 | convolution fusion | flops 1863536640 | bytes 11960864 | tf_op jit(solution)/shard_map/dot_general | solution.py:66
  276.4 22.0 %all-reduce.6 = (f32[96]{0:T(128)}, f32[49]{0:T(128)}) all-reduce(f32[96]{0:T(128)S(1)} %get-tuple-element.38, f32[49]{0:T(128)S(1)} %reduce_sum.201), channel_id=1, replica_groups=mesh['dp'=8,'tensor'=4] {'dp'}, use_global_device_ids=true, to_apply=%region_12.0 | all-reduce | flops 145 | bytes 1160 | tf_op jit(solution)/shard_map/psum | solution.py:114
  298.3 7.6 %concatenate.1 = f32[77,6144]{1,0:T(8,128)} concatenate(f32[21,6144]{1,0:T(8,128)} %collective-permute-done.1, f32[56,6144]{1,0:T(8,128)S(1)} %fusion.1), dimensions={0} | concatenate | bytes 3784704
  311.2 41.1 %all-reduce.5 = (f32[768]{0:T(1024)}, f32[768]{0:T(1024)}, f32[768]{0:T(1024)}, f32[768]{0:T(1024)}, f32[3072]{0:T(1024)S(1)}, /*index=5*/f32[768]{0:T(1024)}) all-reduce(f32[768]{0:T(1024)S(1)} %get-tuple-element.16, f32[768]{0:T(1024)S(1)} %reduce_sum.205, ...), channel_id=1, replica_groups=mesh['dp'=8,'tensor'=4] {'dp','tensor'}, use_global_device_ids=true, to_apply=%region_18.0 | all-reduce | flops 6912 | bytes 55296 | tf_op jit(solution)/shard_map/psum | solution.py:117
  352.9 52.7 %reduce-scatter.9.cloned.1.call-done = f32[96,768]{1,0:T(8,128)} async-done(((f32[3072,768]{1,0:T(8,128)}), f32[96,768]{1,0:T(8,128)}) %reduce-scatter.9.cloned.1.call-update) | async-done | bytes 294928 | tf_op jit(solution)/shard_map/reduce_scatter | solution.py:123
  405.5 140.9 %reduce-scatter.7.cloned.1.call-done = f32[768,96]{0,1:T(8,128)} async-done(((f32[768,3072]{0,1:T(8,128)}), f32[768,96]{0,1:T(8,128)}) %reduce-scatter.7.cloned.1.call-update) | async-done | bytes 294928 | tf_op jit(solution)/shard_map/reduce_scatter | solution.py:122
  (127 shorter events, 39.8 us)
Async XLA Ops:
  7.2 40.2 %copy-start = (bf16[96,196]{1,0:T(8,128)(2,1)S(1)}, bf16[96,196]{1,0:T(8,128)(2,1)}, u32[]{:S(2)}) copy-start(bf16[96,196]{1,0:T(8,128)(2,1)} %param.19) | copy-start | bytes 112900
  7.2 6.6 %copy-start.22 = (bf16[96]{0:T(256)(128)(2,1)S(1)}, bf16[96]{0:T(256)(128)(2,1)}, u32[]{:S(2)}) copy-start(bf16[96]{0:T(256)(128)(2,1)} %param.18) | copy-start | bytes 580
  7.2 35.7 %all-gather.5.cloned.1.call-start = ((), (), s32[]{:S(2)}) async-start(), calls=%async_computation.4 | async-start | bytes 3440640 | tf_op jit(solution)/shard_map/all_gather | solution.py:39
  13.8 164.6 %all-gather.7.cloned.1.call-start = ((), (), s32[]{:S(2)}) async-start(), calls=%async_computation.5 | async-start | bytes 3440640 | tf_op jit(solution)/shard_map/all_gather | solution.py:88
  13.8 31.6 %copy-start.16 = (bf16[196,96]{0,1:T(8,128)(2,1)S(1)}, bf16[196,96]{0,1:T(8,128)(2,1)}, u32[]{:S(2)}) copy-start(bf16[196,96]{0,1:T(8,128)(2,1)} %param.17) | copy-start | bytes 112900
  50.6 55.7 %copy-start.23 = (bf16[49]{0:T(256)(128)(2,1)S(1)}, bf16[49]{0:T(256)(128)(2,1)}, u32[]{:S(2)}) copy-start(bf16[49]{0:T(256)(128)(2,1)} %param.20) | copy-start | bytes 298
  50.6 55.7 %copy-start.18 = (bf16[768]{0:T(1024)(128)(2,1)S(1)}, bf16[768]{0:T(1024)(128)(2,1)}, u32[]{:S(2)}) copy-start(bf16[768]{0:T(1024)(128)(2,1)} %param.23) | copy-start | bytes 4612
  50.6 55.7 %copy-start.19 = (bf16[768]{0:T(1024)(128)(2,1)S(1)}, bf16[768]{0:T(1024)(128)(2,1)}, u32[]{:S(2)}) copy-start(bf16[768]{0:T(1024)(128)(2,1)} %param.24) | copy-start | bytes 4612
  50.6 55.7 %copy-start.17 = (bf16[3072]{0:T(1024)(128)(2,1)S(1)}, bf16[3072]{0:T(1024)(128)(2,1)}, u32[]{:S(2)}) copy-start(bf16[3072]{0:T(1024)(128)(2,1)} %param.26) | copy-start | bytes 18436
  50.6 55.9 %copy-start.21 = (u32[32]{0:T(128)S(1)}, u32[32]{0:T(128)}, u32[]{:S(2)}) copy-start(u32[32]{0:T(128)} %constant.43) | copy-start | bytes 388
  103.5 4.2 collective-permute-start
  123.9 7.1 %slice-start.2 = ((s8[4718592]{0:T(1024)(128)(4,1)}), s8[4194304]{0:T(1024)(128)(4,1)S(1)}, s32[]{:S(2)}) async-start(s8[4718592]{0:T(1024)(128)(4,1)} %bitcast.90), calls=%async_computation.9 | async-start | bytes 8388608
  126.4 4.5 copy-start.12
  126.4 4.6 slice-start.3
  126.4 10.0 %slice-start = ((s8[4718592]{0:T(1024)(128)(4,1)}), s8[4194304]{0:T(1024)(128)(4,1)S(1)}, s32[]{:S(2)}) async-start(s8[4718592]{0:T(1024)(128)(4,1)} %bitcast.88), calls=%async_computation.7 | async-start | bytes 8388608
  131.0 5.4 copy-start.25
  131.0 5.4 copy-start.5
  131.0 5.4 slice-start.1
  144.0 208.9 %all-reduce.10.cloned.1.call-start = ((), (), s32[]{:S(2)}) async-start(), calls=%async_computation.6 | async-start | bytes 393216 | tf_op jit(solution)/shard_map/psum | solution.py:114
  191.6 213.9 %reduce-scatter.9.cloned.1.call-start = ((), (), s32[]{:S(2)}) async-start(), calls=%async_computation.3 | async-start | bytes 9732096 | tf_op jit(solution)/shard_map/reduce_scatter | solution.py:123
  201.0 345.4 %reduce-scatter.7.cloned.1.call-start = ((), (), s32[]{:S(2)}) async-start(), calls=%async_computation.2 | async-start | bytes 9732096 | tf_op jit(solution)/shard_map/reduce_scatter | solution.py:122
  214.4 54.2 %copy-start.6 = (f32[392,768]{1,0:T(8,128)S(1)}, f32[392,768]{1,0:T(8,128)}, u32[]{:S(2)}) copy-start(f32[392,768]{1,0:T(8,128)} %reshape.158) | copy-start | bytes 3612676
  266.3 32.1 %collective-permute-start.1 = (f32[21,6144]{1,0:T(8,128)}, f32[21,6144]{1,0:T(8,128)}, u32[]{:S(2)}, u32[]{:S(2)}) collective-permute-start(f32[21,6144]{1,0:T(8,128)} %slice.1), channel_id=1, source_target_pairs={{0,1},{1,2},{2,3},{4,5},{5,6},{6,7},{8,9},{9,10},{10,11},{12,13},{... | collective-permute-start | bytes 1548296
  309.2 240.4 %copy-start.1 = (bf16[96,196]{1,0:T(8,128)(2,1)S(1)}, bf16[96,196]{1,0:T(8,128)(2,1)}, u32[]{:S(2)}) copy-start(bf16[96,196]{1,0:T(8,128)(2,1)} %param.19) | copy-start | bytes 112900
  (13 other events, 25.6 us)
Sparse Core Ops, SparseCore 0:
  13.9 28.9 all-gather.4
  144.1 34.2 all-gather.6
  191.7 70.1 all-reduce.9
  269.3 136.2 reduce-scatter.8
  411.8 134.5 reduce-scatter.6
where the time goes:
time: 558 us; the launch traced here: 556 us
  waiting for transfers between devices  257 us (46%)
  blocking collectives  166 us (30%)
  matrix products  52.2 us (9%)
  local copies, waits for them, and re-layouts  44.1 us (8%)
  other arithmetic  16.5 us (3%)
  between operations  15.6 us (3%)
    reduce_scatter x1, waiting for transfers between devices, local(): lax.psum_scatter(broaden_grad, ('dp', 'tensor'), scatter_dimension=1, til...  141 us
    unnamed x2, blocking collectives  103 us
    reduce_scatter x1, waiting for transfers between devices, local(): lax.psum_scatter(narrow_grad, ('dp', 'tensor'), scatter_dimension=0, tile...  52.7 us
    unnamed x74, local copies, waits for them, and re-layouts  41.2 us
    psum x1, blocking collectives, local(): lax.psum((lowering_grad, scaling_grad, centering_grad, rescaling_grad, re...  41.1 us
    all_gather x1, waiting for transfers between devices, local(): mixed_all = lax.all_gather(mixed_low, 'tensor', axis=0, tiled=True)  34.2 us
    all_gather x1, waiting for transfers between devices, local(): normed_all = lax.all_gather(normed_local, 'tensor', axis=0, tiled=True)  29.1 us
    psum x1, blocking collectives, local(): lax.psum((expand_grad, uplift_grad, contract_grad, offset_grad), 'dp')  22 us
  transfers between devices with their start and end apart: 7, of which 4 were waited for; matrix products, arithmetic and copies ran while one was open for 17% of the time, Pallas kernels for 0%

commit v1 on v0

--- a/solution.py
+++ b/solution.py
@@ -2,6 +2,22 @@
 import jax.numpy as jnp
 from jax import lax
 from jax.sharding import PartitionSpec as P
+
+
+def collect(x, axis, dim):
+    ways, here, step = (lax.axis_size(axis), lax.axis_index(axis), x.shape[dim])
+    shape = [n * ways if d == dim else n for d, n in enumerate(x.shape)]
+    full = lax.dynamic_update_slice_in_dim(jnp.zeros(shape, x.dtype), x, here * step, axis=dim)
+    going_up = going_down = x
+    for far in range(1, ways // 2 + 1):
+        going_up = lax.ppermute(going_up, axis, [(d, (d + 1) % ways) for d in range(ways)])
+        full = lax.dynamic_update_slice_in_dim(full, going_up, (here - far) % ways * step, axis=dim)
+        if 2 * far < ways:
+            going_down = lax.ppermute(going_down, axis, [(d, (d - 1) % ways) for d in range(ways)])
+            full = lax.dynamic_update_slice_in_dim(
+                full, going_down, (here + far) % ways * step, axis=dim
+            )
+    return full
 
 
 def layer_norm(values, scale_vec, shift_vec):
@@ -36,7 +52,7 @@
         layer_norm, input_float, scaling.astype(jnp.float32), centering.astype(jnp.float32)
     )
     normed_local = normed_first.astype(jnp.bfloat16).reshape(part_rows, columns)
-    normed_all = lax.all_gather(normed_local, "tensor", axis=0, tiled=True)
+    normed_all = collect(normed_local, "tensor", 0)
     token_pre = (
         jnp.einsum("sj,sn->jn", expand, normed_all, preferred_element_type=jnp.float32)
         + uplift.astype(jnp.float32)[:, None]

time: 558 us -> 501 us (0.90)
  waiting for transfers between devices: 257 us -> 170 us
  local copies, waits for them, and re-layouts: 44.1 us -> 59 us
  blocking collectives: 166 us -> 174 us
    reduce_scatter x1, waiting for transfers between devices: 52.7 us -> 0.01 us  [local(): lax.psum_scatter(narrow_grad, ('dp', 'tensor'), scatter_dimension=0, tile...]
    all_gather x1 -> x0, waiting for transfers between devices: 29.1 us -> none  [local(): normed_all = lax.all_gather(normed_local, 'tensor', axis=0, tiled=True)]
    dynamic_update_slice x0 -> x4, local copies, waits for them, and re-layouts: none -> 17.2 us  [the longest x2 8.46 us: collect(): lax.dynamic_update_slice_in_dim(full, going_up, (here - far) % ways * ste...]
    reduce_scatter x1, waiting for transfers between devices: 141 us -> 124 us  [local(): lax.psum_scatter(broaden_grad, ('dp', 'tensor'), scatter_dimension=1, til...]
    ppermute x0 -> x3, waiting for transfers between devices: none -> 13.6 us  [the longest x2 13.6 us: collect(): lax.ppermute(going_up, axis, [(d, (d + 1) % ways) for d in range(ways)])]
    unnamed x2, blocking collectives: 103 us -> 114 us
  transfers between devices with their start and end apart: 7 -> 9, of which waited for: 4 -> 3; matrix products, arithmetic and copies ran while one was open for 17% -> 23% of each run, Pallas kernels for 0% -> 0%
where the time goes in v1:
time: 501 us; the launch traced here: 499 us
  blocking collectives  174 us (35%)
  waiting for transfers between devices  170 us (34%)
  local copies, waits for them, and re-layouts  59 us (12%)
  matrix products  52.6 us (10%)
  between operations  17.4 us (3%)
  other arithmetic  16.5 us (3%)
  starting transfers between devices  9.82 us (2%)
    reduce_scatter x1, waiting for transfers between devices, local(): lax.psum_scatter(broaden_grad, ('dp', 'tensor'), scatter_dimension=1, til...  124 us
    unnamed x2, blocking collectives  114 us
    unnamed x74, local copies, waits for them, and re-layouts  38.5 us
    psum x1, blocking collectives, local(): lax.psum((lowering_grad, scaling_grad, centering_grad, rescaling_grad, re...  38.3 us
    all_gather x1, waiting for transfers between devices, local(): mixed_all = lax.all_gather(mixed_low, 'tensor', axis=0, tiled=True)  32.5 us
    psum x1, blocking collectives, local(): lax.psum((expand_grad, uplift_grad, contract_grad, offset_grad), 'dp')  22 us
    ppermute x2, waiting for transfers between devices, collect(): lax.ppermute(going_up, axis, [(d, (d + 1) % ways) for d in range(ways)])  13.6 us
  transfers between devices with their start and end apart: 9, of which 3 were waited for; matrix products, arithmetic and copies ran while one was open for 23% of the time, Pallas kernels for 0%

profile of v1, /device:TPU:0, one launch (start us, length us, event | category | flops | bytes accessed | tf_op | source)
XLA Modules:
  0.0 499.0 jit_solution(1580848197127059805)
XLA Ops:
  16.8 13.6 %collective-permute-done = bf16[49,6144]{1,0:T(8,128)(2,1)} collective-permute-done((bf16[49,6144]{1,0:T(8,128)(2,1)}, bf16[49,6144]{1,0:T(8,128)(2,1)}, u32[]{:S(2)}, u32[]{:S(2)}) %collective-permute-start) | collective-permute-done | bytes 602144 | tf_op jit(solution)/shard_map/ppermute | solution.py:13
  33.3 4.4 dynamic_update_slice.12
  37.8 4.1 dynamic_update_slice.13
  41.8 4.4 dynamic_update_slice.14
  46.2 4.4 dynamic_update_slice.15
  52.6 3.1 convolution_bitcast_fusion.1
  55.8 54.0 %fusion = f32[56,6144]{1,0:T(8,128)} fusion(f32[196,6144]{1,0:T(8,128)} %convolution_bitcast_fusion.1), kind=kCustom, calls=%all-reduce-scatter | all-reduce-scatter fusion | flops 1376257 | bytes 6193664
  115.1 8.4 %concatenate = f32[77,6144]{1,0:T(8,128)} concatenate(f32[21,6144]{1,0:T(8,128)} %collective-permute-done.3, f32[56,6144]{1,0:T(8,128)} %fusion), dimensions={0} | concatenate | bytes 3784704
  123.5 2.7 dynamic-slice_add_fusion
  126.2 2.6 reshape.158
  133.8 4.5 fusion.52
  138.4 5.5 %convert_reduce_fusion = (f32[3072]{0:T(1024)S(1)}, bf16[392,3072]{1,0:T(8,128)(2,1)S(1)}) fusion(f32[392,3072]{1,0:T(8,128)S(1)} %fusion.52, f32[3072]{0:T(1024)S(1)} %convert_element_type.94, bf16[3072,768]{1,0:T(8,128)(2,1)S(1)} %bitcast.95, bf16[49,8,768]{2,1,0:T(8,128)(2,1)S(1)} %copy-done.12, f32[392]{0:T(512)S(1)} %mul.256), kind=kOutput, calls=%fused_computation.14 | convolution fusion | flops 1878285312 | bytes 12572192 | tf_op jit(solution)/shard_map/rd,kd->rk/dot_general | solution.py:94
  151.8 32.5 %all-gather.3.cloned.1.call-done = bf16[4,49,6144]{2,1,0:T(8,128)(2,1)} async-done(((bf16[1,49,6144]{2,1,0:T(8,128)(2,1)}), bf16[4,49,6144]{2,1,0:T(8,128)(2,1)}) %all-gather.3.cloned.1.call-update) | async-done | bytes 2408464 | tf_op jit(solution)/shard_map/all_gather | solution.py:104
  184.2 4.0 reshape.166
  188.2 4.3 fusion.48
  197.4 9.3 %fusion.41 = f32[3072,768]{1,0:T(8,128)} fusion(bf16[49,8,768]{2,1,0:T(8,128)(2,1)} %param.29, f32[392]{0:T(512)S(1)} %mul.256, f32[392,3072]{1,0:T(8,128)} %copy-done.25, f32[3072]{0:T(1024)S(1)} %convert_element_type.94), kind=kOutput, calls=%fused_computation.69 | convolution fusion | flops 1862633472 | bytes 14870048 | tf_op jit(solution)/shard_map/rk,rd->kd/dot_general | solution.py:92
  207.8 8.0 %fusion.54 = f32[768,3072]{0,1:T(8,128)} fusion(bf16[392,768]{1,0:T(8,128)(2,1)S(1)} %copy-done.15, bf16[392,3072]{1,0:T(8,128)(2,1)} %copy-done.24), kind=kOutput, calls=%fused_computation.87 | convolution fusion | flops 1849688064 | bytes 12447744 | tf_op jit(solution)/shard_map/rd,rk->dk/dot_general | solution.py:97
  217.2 3.1 convolution_bitcast_fusion
  220.3 59.5 %fusion.1 = f32[56,6144]{1,0:T(8,128)S(1)} fusion(f32[196,6144]{1,0:T(8,128)} %convolution_bitcast_fusion), kind=kCustom, calls=%all-reduce-scatter.1 | all-reduce-scatter fusion | flops 1376257 | bytes 6193664
  283.0 8.1 %fusion.26 = bf16[49,8,768]{2,1,0:T(8,128)(2,1)} fusion(bf16[3072,768]{1,0:T(8,128)(2,1)} %param.27, f32[392]{0:T(512)S(1)} %mul.256, f32[768]{0:T(1024)S(1)} %convert_element_type.96, f32[392,768]{1,0:T(8,128)S(1)} %copy-done.6, bf16[49,8,768]{2,1,0:T(8,128)(2,1)S(1)} %copy-done.2, f32[392,3072]{1,0:T(8,128)} %copy-done.25, f32[3072]{0:T(1024)S(1)} %convert_element_type.94), kind=kOutput, calls=%fused_computation.46 | convolution fusion | flops 1863536640 | bytes 11960864 | tf_op jit(solution)/shard_map/dot_general | solution.py:82
  291.0 22.0 %all-reduce.6 = (f32[96]{0:T(128)}, f32[49]{0:T(128)}) all-reduce(f32[96]{0:T(128)S(1)} %get-tuple-element.38, f32[49]{0:T(128)S(1)} %reduce_sum.201), channel_id=1, replica_groups=mesh['dp'=8,'tensor'=4] {'dp'}, use_global_device_ids=true, to_apply=%region_12.13 | all-reduce | flops 145 | bytes 1160 | tf_op jit(solution)/shard_map/psum | solution.py:130
  313.0 7.6 %concatenate.1 = f32[77,6144]{1,0:T(8,128)} concatenate(f32[21,6144]{1,0:T(8,128)} %collective-permute-done.4, f32[56,6144]{1,0:T(8,128)S(1)} %fusion.1), dimensions={0} | concatenate | bytes 3784704
  325.8 38.3 %all-reduce.5 = (f32[768]{0:T(1024)}, f32[768]{0:T(1024)}, f32[768]{0:T(1024)}, f32[768]{0:T(1024)}, f32[3072]{0:T(1024)S(1)}, /*index=5*/f32[768]{0:T(1024)}) all-reduce(f32[768]{0:T(1024)S(1)} %get-tuple-element.16, f32[768]{0:T(1024)S(1)} %reduce_sum.205, ...), channel_id=1, replica_groups=mesh['dp'=8,'tensor'=4] {'dp','tensor'}, use_global_device_ids=true, to_apply=%region_18.19 | all-reduce | flops 6912 | bytes 55296 | tf_op jit(solution)/shard_map/psum | solution.py:133
  364.6 123.8 %reduce-scatter.7.cloned.1.call-done = f32[768,96]{0,1:T(8,128)} async-done(((f32[768,3072]{0,1:T(8,128)}), f32[768,96]{0,1:T(8,128)}) %reduce-scatter.7.cloned.1.call-update) | async-done | bytes 294928 | tf_op jit(solution)/shard_map/reduce_scatter | solution.py:138
  (135 shorter events, 49.6 us)
Async XLA Ops:
  8.0 44.6 %copy-start = (bf16[96,196]{1,0:T(8,128)(2,1)S(1)}, bf16[96,196]{1,0:T(8,128)(2,1)}, u32[]{:S(2)}) copy-start(bf16[96,196]{1,0:T(8,128)(2,1)} %param.19) | copy-start | bytes 112900
  8.0 176.2 %all-gather.3.cloned.1.call-start = ((), (), s32[]{:S(2)}) async-start(), calls=%async_computation.4 | async-start | bytes 3440640 | tf_op jit(solution)/shard_map/all_gather | solution.py:104
  10.7 22.4 %copy-start.22 = (bf16[96]{0:T(256)(128)(2,1)S(1)}, bf16[96]{0:T(256)(128)(2,1)}, u32[]{:S(2)}) copy-start(bf16[96]{0:T(256)(128)(2,1)} %param.18) | copy-start | bytes 580
  14.5 16.0 %collective-permute-start = (bf16[49,6144]{1,0:T(8,128)(2,1)}, bf16[49,6144]{1,0:T(8,128)(2,1)}, u32[]{:S(2)}, u32[]{:S(2)}) collective-permute-start(bf16[49,6144]{1,0:T(8,128)(2,1)} %bitcast.16), channel_id=1, source_target_pairs={{0,1},{1,2},{2,3},{3,0},{4,5},{5,6},{6,7},{7,4},{8,9},{9,10},{10,1... | collective-permute-start | bytes 1806344 | tf_op jit(solution)/shard_map/ppermute | solution.py:13
  14.9 26.9 %collective-permute-start.1 = (bf16[49,6144]{1,0:T(8,128)(2,1)}, bf16[49,6144]{1,0:T(8,128)(2,1)}, u32[]{:S(2)}, u32[]{:S(2)}) collective-permute-start(bf16[49,6144]{1,0:T(8,128)(2,1)} %bitcast.16), channel_id=1, source_target_pairs={{0,3},{1,0},{2,1},{3,2},{4,7},{5,4},{6,5},{7,6},{8,11},{9,8},{10,9... | collective-permute-start | bytes 1806344 | tf_op jit(solution)/shard_map/ppermute | solution.py:16
  30.5 15.7 %collective-permute-start.2 = (bf16[49,6144]{1,0:T(8,128)(2,1)}, bf16[49,6144]{1,0:T(8,128)(2,1)}, u32[]{:S(2)}, u32[]{:S(2)}) collective-permute-start(bf16[49,6144]{1,0:T(8,128)(2,1)} %collective-permute-done), channel_id=1, source_target_pairs={{0,1},{1,2},{2,3},{3,0},{4,5},{5,6},{6,7},{7,4},{8,9},{9,10},{10,1... | collective-permute-start | bytes 1806344 | tf_op jit(solution)/shard_map/ppermute | solution.py:13
  37.7 12.9 %copy-start.16 = (bf16[196,96]{0,1:T(8,128)(2,1)S(1)}, bf16[196,96]{0,1:T(8,128)(2,1)}, u32[]{:S(2)}) copy-start(bf16[196,96]{0,1:T(8,128)(2,1)} %param.17) | copy-start | bytes 112900
  55.7 57.9 %copy-start.23 = (bf16[49]{0:T(256)(128)(2,1)S(1)}, bf16[49]{0:T(256)(128)(2,1)}, u32[]{:S(2)}) copy-start(bf16[49]{0:T(256)(128)(2,1)} %param.20) | copy-start | bytes 298
  55.7 57.9 %copy-start.18 = (bf16[768]{0:T(1024)(128)(2,1)S(1)}, bf16[768]{0:T(1024)(128)(2,1)}, u32[]{:S(2)}) copy-start(bf16[768]{0:T(1024)(128)(2,1)} %param.23) | copy-start | bytes 4612
  55.7 58.0 %copy-start.19 = (bf16[768]{0:T(1024)(128)(2,1)S(1)}, bf16[768]{0:T(1024)(128)(2,1)}, u32[]{:S(2)}) copy-start(bf16[768]{0:T(1024)(128)(2,1)} %param.24) | copy-start | bytes 4612
  55.7 58.0 %copy-start.17 = (bf16[3072]{0:T(1024)(128)(2,1)S(1)}, bf16[3072]{0:T(1024)(128)(2,1)}, u32[]{:S(2)}) copy-start(bf16[3072]{0:T(1024)(128)(2,1)} %param.26) | copy-start | bytes 18436
  55.7 58.1 %copy-start.21 = (u32[32]{0:T(128)S(1)}, u32[32]{0:T(128)}, u32[]{:S(2)}) copy-start(u32[32]{0:T(128)} %constant.82) | copy-start | bytes 388
  110.9 4.2 collective-permute-start.3
  131.2 7.1 %slice-start.2 = ((s8[4718592]{0:T(1024)(128)(4,1)}), s8[4194304]{0:T(1024)(128)(4,1)S(1)}, s32[]{:S(2)}) async-start(s8[4718592]{0:T(1024)(128)(4,1)} %bitcast.94), calls=%async_computation.8 | async-start | bytes 8388608
  133.8 10.1 %slice-start = ((s8[4718592]{0:T(1024)(128)(4,1)}), s8[4194304]{0:T(1024)(128)(4,1)S(1)}, s32[]{:S(2)}) async-start(s8[4718592]{0:T(1024)(128)(4,1)} %bitcast.92), calls=%async_computation.6 | async-start | bytes 8388608
  138.4 5.5 %copy-start.25 = (f32[392,3072]{1,0:T(8,128)}, f32[392,3072]{1,0:T(8,128)S(1)}, u32[]{:S(2)}) copy-start(f32[392,3072]{1,0:T(8,128)S(1)} %fusion.52) | copy-start | bytes 14450692
  138.4 5.5 %copy-start.5 = (f32[392,768]{1,0:T(8,128)S(1)}, f32[392,768]{1,0:T(8,128)}, u32[]{:S(2)}) copy-start(f32[392,768]{1,0:T(8,128)} %reshape.158) | copy-start | bytes 3612676
  138.4 5.5 %slice-start.1 = ((s8[4718592]{0:T(1024)(128)(4,1)}), s8[524288]{0:T(1024)(128)(4,1)S(1)}, s32[]{:S(2)}) async-start(s8[4718592]{0:T(1024)(128)(4,1)} %bitcast.92), calls=%async_computation.7 | async-start | bytes 1048576
  151.5 213.1 %all-reduce.10.cloned.1.call-start = ((), (), s32[]{:S(2)}) async-start(), calls=%async_computation.5 | async-start | bytes 393216 | tf_op jit(solution)/shard_map/psum | solution.py:130
  197.4 167.3 %reduce-scatter.9.cloned.1.call-start = ((), (), s32[]{:S(2)}) async-start(), calls=%async_computation.3 | async-start | bytes 9732096 | tf_op jit(solution)/shard_map/reduce_scatter | solution.py:139
  206.8 281.7 %reduce-scatter.7.cloned.1.call-start = ((), (), s32[]{:S(2)}) async-start(), calls=%async_computation.2 | async-start | bytes 9732096 | tf_op jit(solution)/shard_map/reduce_scatter | solution.py:138
  220.3 62.7 %copy-start.6 = (f32[392,768]{1,0:T(8,128)S(1)}, f32[392,768]{1,0:T(8,128)}, u32[]{:S(2)}) copy-start(f32[392,768]{1,0:T(8,128)} %reshape.158) | copy-start | bytes 3612676
  280.6 32.4 %collective-permute-start.4 = (f32[21,6144]{1,0:T(8,128)}, f32[21,6144]{1,0:T(8,128)}, u32[]{:S(2)}, u32[]{:S(2)}) collective-permute-start(f32[21,6144]{1,0:T(8,128)} %slice.1), channel_id=1, source_target_pairs={{0,1},{1,2},{2,3},{4,5},{5,6},{6,7},{8,9},{9,10},{10,11},{12,13},{... | collective-permute-start | bytes 1548296
  323.9 167.7 %copy-start.1 = (bf16[96,196]{1,0:T(8,128)(2,1)S(1)}, bf16[96,196]{1,0:T(8,128)(2,1)}, u32[]{:S(2)}) copy-start(bf16[96,196]{1,0:T(8,128)(2,1)} %param.19) | copy-start | bytes 112900
  (15 other events, 34.8 us)
Sparse Core Ops, SparseCore 0:
  151.6 32.5 all-gather.2
  197.5 79.9 all-reduce.9
Sparse Core Ops, SparseCore 1:
  206.9 140.6 reduce-scatter.8
  353.8 134.6 reduce-scatter.6
